TPU v7x, 512 devices: a whole 4x8x8 slice. The times are simulated.
512 devices in a mesh: seq: 128 (over y, z, core), mp: 4 (over x).
Axes of the slice: x: 4, y: 8, z: 8, core: 2. Of those that a mesh axis runs over, the one named last changes fastest.
Arguments:
- fresh_queries: bfloat16 [8192, 2048], P('seq', 'mp'), may hold values from -120 to 120
- fresh_keys: bfloat16 [8192, 1024], P('seq', 'mp'), may hold values from -6 to 6
- fresh_values: bfloat16 [8192, 1024], P('seq', 'mp'), may hold values from -6 to 6
- cache: bfloat16 [2, 8192, 1024], P(None, 'seq', 'mp'), may hold values from -6 to 6
- pool_root: int32 [128, 32], replicated, may hold values from 0 to 31
- branch_owner: int32 [128], replicated, may hold values from 0 to 127, each once
- branch_len: int32 [128], replicated, may hold values from 1 to 32, 2048 in all
- branch_root: int32 [128], replicated, may hold values from 0 to 31
- request_branch: int32 [128, 4], P('seq'), may hold values from 0 to 127
- token_request: int32 [128, 64], P('seq'), may hold values from 0 to 3, never falling along the last dimension, each value on 1 to 32 neighbouring positions
- residual: bfloat16 [8192, 2048], P('seq'), may hold values from -1.5 to 1.5
- wo_t: bfloat16 [2048, 2048], P('seq', 'mp'), may hold values from -0.125 to 0.125
- norm_gain: float32 [2048], replicated, may hold values from 0.1 to 1.9
- w_qkv: bfloat16 [2048, 4096], P('seq', 'mp'), may hold values from -0.125 to 0.125
Outputs:
- attn: bfloat16 [8192, 2048], P('seq', 'mp')
- stream: bfloat16 [8192, 2048], P('seq')
- qkv_next: bfloat16 [8192, 4096], P('seq', 'mp')
Inputs may be any that keep to these rules, and one draw needn't show every extreme that they name: `token_request`: in each index's row the request number never falls, and each request has 1 to 32 tokens. `branch_owner`: each index of seq holds exactly one branch. `branch_len`: the longest branch has 32 rows.
All inputs are finite; a program needn't handle non-finite values.
Results may differ from a plain program's by a relative error of at most 0.018.
Values may be sent and summed in bfloat16 or wider, within the bound.
A program may use at most 64 MiB of HBM per device.

v0:
```python
import jax
import jax.numpy as jnp
from jax import lax
from jax.sharding import PartitionSpec as P

QUERY_HEADS = 16
KEY_VALUE_HEADS = 8
HEAD_SIZE = 128


def cache_tags(pool_root, branch_owner, branch_len, root_count, slot_count):
    owner_count = pool_root.shape[0]
    branch_count = branch_owner.shape[0]
    branch_ids = jnp.arange(branch_count, dtype=jnp.int32)
    owner_ids = jnp.arange(owner_count, dtype=jnp.int32)
    owned = jnp.sum(
        jnp.where(branch_owner[None, :] == owner_ids[:, None], branch_ids[None, :], 0), axis=1
    )
    owned_length = jnp.sum(
        jnp.where(branch_ids[None, :] == owned[:, None], branch_len[None, :], 0), axis=1
    )
    slot_ids = jnp.arange(slot_count, dtype=jnp.int32)
    branch_tags = jnp.where(
        slot_ids[None, :] < owned_length[:, None], root_count + owned[:, None], -1
    )
    return jnp.concatenate([pool_root, branch_tags], axis=1).reshape(-1)


def absorb(running, query_rows, key_row_block, value_rows, visible, score_scale):
    peak_old, total, mixed = running
    scores = (
        jnp.einsum("tkgd,rkd->tkgr", query_rows, key_row_block, preferred_element_type=jnp.float32)
        * score_scale
    )
    seen = visible[:, None, None, :]
    peak_new = jnp.maximum(peak_old, jnp.max(jnp.where(seen, scores, -jnp.inf), axis=-1))
    factor = jnp.exp(peak_old - peak_new)
    weights_full = jnp.where(seen, jnp.exp(scores - peak_new[..., None]), 0.0)
    total = total * factor + jnp.sum(weights_full, axis=-1)
    mixed = mixed * factor[..., None] + jnp.einsum(
        "tkgr,rkd->tkgd",
        weights_full.astype(jnp.bfloat16),
        value_rows,
        preferred_element_type=jnp.float32,
    )
    return (peak_new, total, mixed)


def on_device(
    fresh_queries,
    fresh_keys,
    fresh_values,
    cache,
    pool_root,
    branch_owner,
    branch_len,
    branch_root,
    request_branch,
    token_request,
    residual,
    wo_t,
    norm_gain,
    w_qkv,
):
    seq_count = lax.axis_size("seq")
    root_count = seq_count // 4
    tok_rows = fresh_queries.shape[0]
    kv_local = fresh_keys.shape[1] // HEAD_SIZE
    query_groups = QUERY_HEADS // KEY_VALUE_HEADS
    score_scale = HEAD_SIZE ** (-0.5)
    slot_count = cache.shape[1] - pool_root.shape[1]
    tags = cache_tags(pool_root, branch_owner, branch_len, root_count, slot_count)
    requests = token_request[0]
    local_branches = request_branch[0]
    request_ids = jnp.arange(local_branches.shape[0], dtype=jnp.int32)
    token_branch = jnp.sum(
        jnp.where(requests[:, None] == request_ids[None, :], local_branches[None, :], 0), axis=1
    )
    branch_ids = jnp.arange(branch_root.shape[0], dtype=jnp.int32)
    token_root = jnp.sum(
        jnp.where(token_branch[:, None] == branch_ids[None, :], branch_root[None, :], 0), axis=1
    )
    query_rows = fresh_queries.reshape(tok_rows, kv_local, query_groups, HEAD_SIZE)
    incoming_keys = fresh_keys.reshape(tok_rows, kv_local, HEAD_SIZE)
    incoming_values = fresh_values.reshape(tok_rows, kv_local, HEAD_SIZE)
    positions = jnp.arange(tok_rows, dtype=jnp.int32)
    own_visible = (requests[None, :] == requests[:, None]) & (
        positions[None, :] <= positions[:, None]
    )
    start_state = (
        jnp.full((tok_rows, kv_local, query_groups), -jnp.inf, jnp.float32),
        jnp.zeros((tok_rows, kv_local, query_groups), jnp.float32),
        jnp.zeros((tok_rows, kv_local, query_groups, HEAD_SIZE), jnp.float32),
    )
    start_state = absorb(
        start_state, query_rows, incoming_keys, incoming_values, own_visible, score_scale
    )
    state = start_state
    piece = lax.all_gather(cache, "seq", axis=1, tiled=True)
    rows = piece.shape[1]
    block = 512
    key_blocks = piece[0].reshape(rows // block, block, kv_local, HEAD_SIZE)
    value_blocks = piece[1].reshape(rows // block, block, kv_local, HEAD_SIZE)
    tag_blocks = tags.reshape(rows // block, block)

    def one_block(running, parts):
        key_row_block, value_rows, tag_rows = parts
        visible = (tag_rows[None, :] == token_root[:, None]) | (
            tag_rows[None, :] == root_count + token_branch[:, None]
        )
        updated = absorb(running, query_rows, key_row_block, value_rows, visible, score_scale)
        return (updated, None)

    state, unused = lax.scan(one_block, state, (key_blocks, value_blocks, tag_blocks))
    peak_final, total_final, mixed_final = state
    attn = (
        (mixed_final / total_final[..., None])
        .reshape(tok_rows, kv_local * query_groups * HEAD_SIZE)
        .astype(jnp.bfloat16)
    )
    partial_value = lax.dot_general(
        attn,
        lax.all_gather(wo_t, "seq", axis=0, tiled=True),
        (((1,), (1,)), ((), ())),
        preferred_element_type=jnp.float32,
    )
    summed = lax.psum(partial_value.astype(jnp.bfloat16), "mp").astype(jnp.float32)
    stream = (residual.astype(jnp.float32) + summed).astype(jnp.bfloat16)
    widened = stream.astype(jnp.float32)
    mean_square = jnp.mean(widened * widened, axis=-1, keepdims=True)
    normed = (widened * lax.rsqrt(mean_square + 1e-06) * norm_gain[None, :]).astype(jnp.bfloat16)
    qkv_sum = jnp.dot(
        normed, lax.all_gather(w_qkv, "seq", axis=0, tiled=True), preferred_element_type=jnp.float32
    )
    return (attn, stream, qkv_sum.astype(jnp.bfloat16))


def solution(mesh):
    return jax.shard_map(
        on_device,
        mesh=mesh,
        in_specs=(
            P("seq", "mp"),
            P("seq", "mp"),
            P("seq", "mp"),
            P(None, "seq", "mp"),
            P(),
            P(),
            P(),
            P(),
            P("seq", None),
            P("seq", None),
            P("seq", None),
            P("seq", "mp"),
            P(),
            P("seq", "mp"),
        ),
        out_specs=(P("seq", "mp"), P("seq", None), P("seq", "mp")),
        check_vma=False,
    )
```

profile of v0, /device:TPU:1, one launch (start us, length us, event | category | flops | bytes accessed | tf_op | source)
XLA Modules:
  0.0 339.6 jit_solution(17679690994480268077)
XLA Ops:
  16.6 88.7 %all-gather.4.cloned.1.call-done = bf16[2,8192,256]{2,1,0:T(8,128)(2,1)} async-done(((bf16[2,64,256]{2,1,0:T(8,128)(2,1)}), bf16[2,8192,256]{2,1,0:T(8,128)(2,1)}) %all-gather.4.cloned.1.call-update) | async-done | bytes 8388624 | tf_op jit(solution)/shard_map/all_gather | solution.py:99
  105.3 5.7 %fusion.30 = (bf16[1,8192,256]{2,1,0:T(8,128)(2,1)}, bf16[1,8192,256]{2,1,0:T(8,128)(2,1)}) fusion(bf16[2,8192,256]{2,1,0:T(8,128)(2,1)} %all-gather.4.cloned.1.call-done), kind=kLoop, calls=%fused_computation.64 | loop fusion | bytes 16777216 | tf_op jit(solution)/shard_map/slice | solution.py:103
  111.0 6.9 %reshape.143 = bf16[16,512,2,128]{3,2,1,0:T(2,128)(2,1)} reshape(bf16[1,8192,256]{2,1,0:T(8,128)(2,1)} %get-tuple-element.107) | data formatting | bytes 8388608 | tf_op jit(solution)/shard_map/reshape;squeeze | solution.py:102
  118.0 6.9 %reshape.144 = bf16[16,512,2,128]{3,2,1,0:T(2,128)(2,1)} reshape(bf16[1,8192,256]{2,1,0:T(8,128)(2,1)} %get-tuple-element.106) | data formatting | bytes 8388608 | tf_op jit(solution)/shard_map/reshape;squeeze | solution.py:103
  124.9 39.2 %while.14 = (s32[]{:T(128)}, f32[64,2,2]{0,2,1:T(2,128)S(1)}, f32[64,2,2]{0,2,1:T(2,128)S(1)}, f32[64,2,2,128]{3,0,2,1:T(8,128)S(1)}, s32[16,512]{1,0:T(8,128)S(...) while((s32[]{:T(128)}, f32[64,2,2]{0,2,1:T(2,128)S(1)}, ...), condition=%wide.region_9.10_spmd, body=%wide.region_6.9_spmd.sunk | while | flops 68452928 | bytes 3628149 | solution.py:114
  125.0 1.4 constant_dynamic-slice_fusion.6
  127.5 1.4 constant_dynamic-slice_fusion.6
  129.9 1.4 constant_dynamic-slice_fusion.6
  132.4 1.4 constant_dynamic-slice_fusion.6
  134.8 1.4 constant_dynamic-slice_fusion.6
  137.3 1.4 constant_dynamic-slice_fusion.6
  139.7 1.4 constant_dynamic-slice_fusion.6
  142.2 1.4 constant_dynamic-slice_fusion.6
  144.6 1.4 constant_dynamic-slice_fusion.6
  147.1 1.4 constant_dynamic-slice_fusion.6
  149.5 1.4 constant_dynamic-slice_fusion.6
  152.0 1.4 constant_dynamic-slice_fusion.6
  154.4 1.4 constant_dynamic-slice_fusion.6
  159.3 1.4 constant_dynamic-slice_fusion.6
  164.3 23.8 %all-gather.6.cloned.1.call-done = bf16[2048,512]{1,0:T(8,128)(2,1)} async-done(((bf16[16,512]{1,0:T(8,128)(2,1)}), bf16[2048,512]{1,0:T(8,128)(2,1)}) %all-gather.6.cloned.1.call-update) | async-done | bytes 2097168 | tf_op jit(solution)/shard_map/all_gather | solution.py:123
  188.1 3.0 convolution_convert_fusion
  191.8 46.3 %all-reduce.2.cloned.1.call-done = bf16[64,2048]{1,0:T(8,128)(2,1)} async-done(((bf16[64,2048]{1,0:T(8,128)(2,1)}), bf16[64,2048]{1,0:T(8,128)(2,1)}) %all-reduce.2.cloned.1.call-update) | async-done | bytes 262160 | tf_op jit(solution)/shard_map/psum | solution.py:127
  239.3 90.1 %all-gather.8.cloned.1.call-done = bf16[2048,1024]{1,0:T(8,128)(2,1)} async-done(((bf16[16,1024]{1,0:T(8,128)(2,1)}), bf16[2048,1024]{1,0:T(8,128)(2,1)}) %all-gather.8.cloned.1.call-update) | async-done | bytes 4194320 | tf_op jit(solution)/shard_map/all_gather | solution.py:133
  329.3 3.7 %convolution_convert_fusion.1 = bf16[64,1024]{1,0:T(8,128)(2,1)} fusion(bf16[2048,1024]{1,0:T(8,128)(2,1)} %all-gather.8.cloned.1.call-done, bf16[64,2048]{1,0:T(8,128)(2,1)S(1)} %get-tuple-element.101, f32[2048]{0:T(1024)S(1)} %copy-done.3, f32[64]{0:T(128)S(1)} %add_rsqrt_fusion), kind=kOutput, calls=%fused_computation.22 | convolution fusion | flops 269025280 | bytes 4595968 | tf_op jit(solution)/shard_map/dot_general | solution.py:132
  (185 shorter events, 29.8 us)
Async XLA Ops:
  7.2 98.1 %all-gather.4.cloned.1.call-start = ((), (), s32[]{:S(2)}) async-start(), calls=%async_computation | async-start | bytes 8454144 | tf_op jit(solution)/shard_map/all_gather | solution.py:99
  7.9 180.2 %all-gather.6.cloned.1.call-start = ((), (), s32[]{:S(2)}) async-start(), calls=%async_computation.1 | async-start | bytes 2113536 | tf_op jit(solution)/shard_map/all_gather | solution.py:123
  8.6 229.4 %all-reduce.2.cloned.1.call-start = ((), (), s32[]{:S(2)}) async-start(), calls=%async_computation.2 | async-start | bytes 524288 | tf_op jit(solution)/shard_map/psum | solution.py:127
  124.9 113.2 %copy-start.2 = (bf16[64,2048]{1,0:T(8,128)(2,1)S(1)}, bf16[64,2048]{1,0:T(8,128)(2,1)}, u32[]{:S(2)}) copy-start(bf16[64,2048]{1,0:T(8,128)(2,1)} %param.26) | copy-start | bytes 786436
  124.9 204.4 %copy-start.3 = (f32[2048]{0:T(1024)S(1)}, f32[2048]{0:T(1024)}, u32[]{:S(2)}) copy-start(f32[2048]{0:T(1024)} %param.28) | copy-start | bytes 24580
  164.3 168.7 %copy-start.1 = (bf16[64,512]{1,0:T(8,128)(2,1)}, bf16[64,512]{1,0:T(8,128)(2,1)S(1)}, u32[]{:S(2)}) copy-start(bf16[64,512]{1,0:T(8,128)(2,1)S(1)} %convert_element_type.35) | copy-start | bytes 196612
  191.2 138.1 %all-gather.8.cloned.1.call-start = ((), (), s32[]{:S(2)}) async-start(), calls=%async_computation.3 | async-start | bytes 4227072 | tf_op jit(solution)/shard_map/all_gather | solution.py:133
  239.2 93.8 %copy-start = (bf16[64,2048]{1,0:T(8,128)(2,1)}, bf16[64,2048]{1,0:T(8,128)(2,1)S(1)}, u32[]{:S(2)}) copy-start(bf16[64,2048]{1,0:T(8,128)(2,1)S(1)} %get-tuple-element.101) | copy-start | bytes 786436
Sparse Core Ops, SparseCore 0:
  11.2 94.0 all-gather.3
  108.4 79.6 all-gather.5
  191.3 46.7 all-reduce.1
  241.5 87.7 all-gather.7
where the time goes:
time: 341 us; the launch traced here: 340 us
  waiting for transfers between devices  251 us (74%)
  local copies, waits for them, and re-layouts  44.9 us (13%)
  matrix products  17.1 us (5%)
  between operations  13.9 us (4%)
  other arithmetic  11.8 us (3%)
    all_gather x1, waiting for transfers between devices, on_device(): lax.all_gather(w_qkv, 'seq', axis=0, tiled=True)  90.1 us
    all_gather x1, waiting for transfers between devices, on_device(): piece = lax.all_gather(cache, 'seq', axis=1, tiled=True)  88.7 us
    psum x1, waiting for transfers between devices, on_device(): lax.psum(partial_value.astype(jnp.bfloat16), 'mp').astype(jnp.float32)  46.3 us
    all_gather x1, waiting for transfers between devices, on_device(): lax.all_gather(wo_t, 'seq', axis=0, tiled=True)  23.8 us
    dynamic_slice x32, local copies, waits for them, and re-layouts, on_device(): lax.scan(one_block, state, (key_blocks, value_blocks, tag_blocks))  22.5 us
    another operation x1, local copies, waits for them, and re-layouts, on_device(): value_blocks = piece[1].reshape(rows // block, block, kv_local, HEAD_SIZE)  6.94 us
    another operation x1, local copies, waits for them, and re-layouts, on_device(): key_blocks = piece[0].reshape(rows // block, block, kv_local, HEAD_SIZE)  6.93 us
  transfers between devices with their start and end apart: 4, of which 4 were waited for; matrix products, arithmetic and copies ran while one was open for 20% of the time, Pallas kernels for 0%

commit v1 on v0

--- a/solution.py
+++ b/solution.py
@@ -2,6 +2,7 @@
 import jax.numpy as jnp
 from jax import lax
 from jax.sharding import PartitionSpec as P
+from jax.lax import all_gather
 
 QUERY_HEADS = 16
 KEY_VALUE_HEADS = 8
@@ -124,7 +125,12 @@
         (((1,), (1,)), ((), ())),
         preferred_element_type=jnp.float32,
     )
-    summed = lax.psum(partial_value.astype(jnp.bfloat16), "mp").astype(jnp.float32)
+
+    def name_slices(x_part, mesh_ax):
+        o_now = all_gather(x_part, mesh_ax).sum(axis=0)
+        return o_now
+
+    summed = name_slices(partial_value.astype(jnp.bfloat16), "mp").astype(jnp.float32)
     stream = (residual.astype(jnp.float32) + summed).astype(jnp.bfloat16)
     widened = stream.astype(jnp.float32)
     mean_square = jnp.mean(widened * widened, axis=-1, keepdims=True)

time: 341 us -> 317 us (0.930)
  waiting for transfers between devices: 251 us -> 227 us
    psum x1 -> x0, waiting for transfers between devices: 46.3 us -> none  [on_device(): lax.psum(partial_value.astype(jnp.bfloat16), 'mp').astype(jnp.float32)]
    all_gather x0 -> x1, waiting for transfers between devices: none -> 24.5 us  [name_slices(): o_now = all_gather(x_part, mesh_ax).sum(axis=0)]
  transfers between devices with their start and end apart: 4 -> 4, of which waited for: 4 -> 4; matrix products, arithmetic and copies ran while one was open for 20% -> 21% of each run, Pallas kernels for 0% -> 0%
where the time goes in v1:
time: 317 us; the launch traced here: 316 us
  waiting for transfers between devices  227 us (72%)
  local copies, waits for them, and re-layouts  44.9 us (14%)
  matrix products  17.1 us (5%)
  between operations  13.9 us (4%)
  other arithmetic  12.2 us (4%)
    all_gather x1, waiting for transfers between devices, on_device(): piece = lax.all_gather(cache, 'seq', axis=1, tiled=True)  88.7 us
    all_gather x1, waiting for transfers between devices, on_device(): lax.all_gather(w_qkv, 'seq', axis=0, tiled=True)  87.8 us
    all_gather x1, waiting for transfers between devices, name_slices(): o_now = all_gather(x_part, mesh_ax).sum(axis=0)  24.5 us
    all_gather x1, waiting for transfers between devices, on_device(): lax.all_gather(wo_t, 'seq', axis=0, tiled=True)  23.8 us
    dynamic_slice x32, local copies, waits for them, and re-layouts, on_device(): lax.scan(one_block, state, (key_blocks, value_blocks, tag_blocks))  22.5 us
    another operation x1, local copies, waits for them, and re-layouts, on_device(): value_blocks = piece[1].reshape(rows // block, block, kv_local, HEAD_SIZE)  6.94 us
    another operation x1, local copies, waits for them, and re-layouts, on_device(): key_blocks = piece[0].reshape(rows // block, block, kv_local, HEAD_SIZE)  6.93 us
  transfers between devices with their start and end apart: 4, of which 4 were waited for; matrix products, arithmetic and copies ran while one was open for 21% of the time, Pallas kernels for 0%

profile of v1, /device:TPU:1, one launch (start us, length us, event | category | flops | bytes accessed | tf_op | source)
XLA Modules:
  0.0 315.9 jit_solution(10277070558923110238)
XLA Ops:
  16.6 88.7 %all-gather.6.cloned.1.call-done = bf16[2,8192,256]{2,1,0:T(8,128)(2,1)} async-done(((bf16[2,64,256]{2,1,0:T(8,128)(2,1)}), bf16[2,8192,256]{2,1,0:T(8,128)(2,1)}) %all-gather.6.cloned.1.call-update) | async-done | bytes 8388624 | tf_op jit(solution)/shard_map/all_gather | solution.py:100
  105.3 5.7 %fusion.30 = (bf16[1,8192,256]{2,1,0:T(8,128)(2,1)}, bf16[1,8192,256]{2,1,0:T(8,128)(2,1)}) fusion(bf16[2,8192,256]{2,1,0:T(8,128)(2,1)} %all-gather.6.cloned.1.call-done), kind=kLoop, calls=%fused_computation.64 | loop fusion | bytes 16777216 | tf_op jit(solution)/shard_map/slice | solution.py:104
  111.0 6.9 %reshape.144 = bf16[16,512,2,128]{3,2,1,0:T(2,128)(2,1)} reshape(bf16[1,8192,256]{2,1,0:T(8,128)(2,1)} %get-tuple-element.107) | data formatting | bytes 8388608 | tf_op jit(solution)/shard_map/reshape;squeeze | solution.py:103
  118.0 6.9 %reshape.145 = bf16[16,512,2,128]{3,2,1,0:T(2,128)(2,1)} reshape(bf16[1,8192,256]{2,1,0:T(8,128)(2,1)} %get-tuple-element.106) | data formatting | bytes 8388608 | tf_op jit(solution)/shard_map/reshape;squeeze | solution.py:104
  124.9 39.2 %while.14 = (s32[]{:T(128)}, f32[64,2,2]{0,2,1:T(2,128)S(1)}, f32[64,2,2]{0,2,1:T(2,128)S(1)}, f32[64,2,2,128]{3,0,2,1:T(8,128)S(1)}, s32[16,512]{1,0:T(8,128)S(...) while((s32[]{:T(128)}, f32[64,2,2]{0,2,1:T(2,128)S(1)}, ...), condition=%wide.region_9.10_spmd, body=%wide.region_6.9_spmd.sunk | while | flops 68452928 | bytes 3628149 | solution.py:115
  125.0 1.4 constant_dynamic-slice_fusion.6
  127.5 1.4 constant_dynamic-slice_fusion.6
  129.9 1.4 constant_dynamic-slice_fusion.6
  132.4 1.4 constant_dynamic-slice_fusion.6
  134.8 1.4 constant_dynamic-slice_fusion.6
  137.3 1.4 constant_dynamic-slice_fusion.6
  139.7 1.4 constant_dynamic-slice_fusion.6
  142.2 1.4 constant_dynamic-slice_fusion.6
  144.6 1.4 constant_dynamic-slice_fusion.6
  147.1 1.4 constant_dynamic-slice_fusion.6
  149.5 1.4 constant_dynamic-slice_fusion.6
  152.0 1.4 constant_dynamic-slice_fusion.6
  159.3 1.4 constant_dynamic-slice_fusion.6
  164.4 23.8 %all-gather.8.cloned.1.call-done = bf16[2048,512]{1,0:T(8,128)(2,1)} async-done(((bf16[16,512]{1,0:T(8,128)(2,1)}), bf16[2048,512]{1,0:T(8,128)(2,1)}) %all-gather.8.cloned.1.call-update) | async-done | bytes 2097168 | tf_op jit(solution)/shard_map/all_gather | solution.py:124
  188.1 3.0 convolution_convert_fusion
  191.8 24.5 %all-gather.12.cloned.1.call-done = bf16[256,2048]{1,0:T(8,128)(2,1)} async-done(((bf16[64,2048]{1,0:T(8,128)(2,1)}), bf16[256,2048]{1,0:T(8,128)(2,1)}) %all-gather.12.cloned.1.call-update) | async-done | bytes 1048592 | tf_op jit(solution)/shard_map/all_gather | solution.py:130
  216.2 1.4 reduce_sum.80
  217.9 87.8 %all-gather.10.cloned.1.call-done = bf16[2048,1024]{1,0:T(8,128)(2,1)} async-done(((bf16[16,1024]{1,0:T(8,128)(2,1)}), bf16[2048,1024]{1,0:T(8,128)(2,1)}) %all-gather.10.cloned.1.call-update) | async-done | bytes 4194320 | tf_op jit(solution)/shard_map/all_gather | solution.py:139
  305.6 3.7 %convolution_convert_fusion.1 = bf16[64,1024]{1,0:T(8,128)(2,1)} fusion(bf16[2048,1024]{1,0:T(8,128)(2,1)} %all-gather.10.cloned.1.call-done, bf16[64,2048]{1,0:T(8,128)(2,1)S(1)} %get-tuple-element.101, f32[2048]{0:T(1024)S(1)} %copy-done.3, f32[64]{0:T(128)S(1)} %add_rsqrt_fusion), kind=kOutput, calls=%fused_computation.22 | convolution fusion | flops 269025280 | bytes 4595968 | tf_op jit(solution)/shard_map/dot_general | solution.py:138
  (186 shorter events, 30.3 us)
Async XLA Ops:
  7.2 98.1 %all-gather.6.cloned.1.call-start = ((), (), s32[]{:S(2)}) async-start(), calls=%async_computation | async-start | bytes 8454144 | tf_op jit(solution)/shard_map/all_gather | solution.py:100
  7.9 180.2 %all-gather.8.cloned.1.call-start = ((), (), s32[]{:S(2)}) async-start(), calls=%async_computation.1 | async-start | bytes 2113536 | tf_op jit(solution)/shard_map/all_gather | solution.py:124
  8.6 207.6 %all-gather.12.cloned.1.call-start = ((), (), s32[]{:S(2)}) async-start(), calls=%async_computation.3 | async-start | bytes 1310720 | tf_op jit(solution)/shard_map/all_gather | solution.py:130
  164.1 53.6 %copy-start.2 = (bf16[64,2048]{1,0:T(8,128)(2,1)S(1)}, bf16[64,2048]{1,0:T(8,128)(2,1)}, u32[]{:S(2)}) copy-start(bf16[64,2048]{1,0:T(8,128)(2,1)} %param.26) | copy-start | bytes 786436
  164.1 141.5 %copy-start.3 = (f32[2048]{0:T(1024)S(1)}, f32[2048]{0:T(1024)}, u32[]{:S(2)}) copy-start(f32[2048]{0:T(1024)} %param.28) | copy-start | bytes 24580
  164.3 145.0 %copy-start.1 = (bf16[64,512]{1,0:T(8,128)(2,1)}, bf16[64,512]{1,0:T(8,128)(2,1)S(1)}, u32[]{:S(2)}) copy-start(bf16[64,512]{1,0:T(8,128)(2,1)S(1)} %convert_element_type.37) | copy-start | bytes 196612
  191.2 114.4 %all-gather.10.cloned.1.call-start = ((), (), s32[]{:S(2)}) async-start(), calls=%async_computation.2 | async-start | bytes 4227072 | tf_op jit(solution)/shard_map/all_gather | solution.py:139
  217.9 91.5 %copy-start = (bf16[64,2048]{1,0:T(8,128)(2,1)}, bf16[64,2048]{1,0:T(8,128)(2,1)S(1)}, u32[]{:S(2)}) copy-start(bf16[64,2048]{1,0:T(8,128)(2,1)S(1)} %get-tuple-element.101) | copy-start | bytes 786436
Sparse Core Ops, SparseCore 0:
  11.2 94.0 all-gather.5
  108.4 79.6 all-gather.7
  191.3 24.8 all-gather.11
  219.2 86.3 all-gather.9
